TPU v7x, 32 devices: a whole 2x2x4 slice. The times are simulated.
32 devices in a mesh: skyx: 2 (over y), skyy: 4 (over x, core), freq: 4 (over z).
Axes of the slice: x: 2, y: 2, z: 4, core: 2. Of those that a mesh axis runs over, the one named last changes fastest.
Arguments:
- field: float32 [512, 8, 512], P('freq', 'skyx', 'skyy'), may hold values from -6 to 6
- noise: float32 [512, 8, 512], P('freq', 'skyx', 'skyy'), may hold values from -1.2 to 1.2
- step_size: float32 [512], P('freq'), may hold values from 0.35 to 0.6
- w_first: bfloat16 [3, 3, 64, 1], replicated, may hold values from -2 to 2
- w_second: bfloat16 [3, 3, 64, 64], replicated, may hold values from -0.25 to 0.25
- w_third: bfloat16 [3, 3, 64, 64], replicated, may hold values from -0.25 to 0.25
- w_last: bfloat16 [3, 3, 1, 64], replicated, may hold values from -0.25 to 0.25
- observed: float32 [512, 8, 512], P(None, ('skyx', 'freq'), 'skyy'), may hold values from -6 to 6
- inv_variance: float32 [512, 8, 512], P(None, ('skyx', 'freq'), 'skyy'), may hold values from 0.3 to 3
- offsets: int32 [8], P(('skyx', 'freq')), may hold values from 0 to 512
- beam_table: float32 [1024, 31], replicated, may hold values from -1 to 1
- kbin: int32 [8, 512], P(('skyx', 'freq'), 'skyy'), may hold values from 0 to 7
- wedge_taps: float32 [8, 31], replicated, may hold values from -1 to 1
Outputs:
- next_field: float32 [512, 8, 512], P('freq', 'skyx', 'skyy')
Inputs may be any that keep to these rules, and one draw needn't show every extreme that they name: `offsets`: every offset plus 512 is at most 1024.
All inputs are finite; a program needn't handle non-finite values.
Results may differ from a plain program's by a relative error of at most 0.0045.
Values may be sent and summed in bfloat16 or wider, within the bound.
No kernel may reach another device: no remote copies, remote signals or barrier semaphores. Data moves between devices by JAX's collectives and lax.ppermute only.
A program may use at most 448 MiB of HBM per device.

v0:
```python
import jax
import jax.numpy as jnp
from jax import lax
from jax.sharding import PartitionSpec as P

TAPS = 31
KBINS = 8


def padded_2(block, sides, width):
    for axis, dim in sides:
        count = lax.axis_size(axis)
        forward = [(i, i + 1) for i in range(count - 1)]
        backward = [(target, source) for source, target in forward]
        low = lax.ppermute(
            lax.slice_in_dim(block, block.shape[dim] - width, None, axis=dim), axis, forward
        )
        high = lax.ppermute(lax.slice_in_dim(block, 0, width, axis=dim), axis, backward)
        block = jnp.concatenate([low, block, high], axis=dim)
    return block


def conv_local(padded, kernel):
    height = padded.shape[2] - 2
    width = padded.shape[3] - 2
    total = None
    for row_tap in range(3):
        for col_tap in range(3):
            window = padded[:, :, row_tap : row_tap + height, col_tap : col_tap + width]
            term = jnp.einsum(
                "oc,fchw->fohw",
                kernel[row_tap, col_tap],
                window,
                preferred_element_type=jnp.float32,
            )
            total = term if total is None else total + term
    return total


def with_rim(values):
    return padded_2(values, (("skyx", 2), ("skyy", 3)), 1)


def per_device(
    field,
    noise,
    step_size,
    w_first,
    w_second,
    w_third,
    w_last,
    observed,
    inv_variance,
    offsets,
    beam_table,
    kbin,
    wedge_taps,
):
    xb = field.astype(jnp.bfloat16)
    kernels = (w_first, w_second, w_third)
    hidden = xb[:, None]
    for kernel in kernels:
        hidden = jax.nn.silu(conv_local(with_rim(hidden), kernel)).astype(jnp.bfloat16)
    score = conv_local(with_rim(hidden), w_last)[:, 0]
    spectra = lax.all_to_all(xb, "freq", split_axis=1, concat_axis=0, tiled=True)
    chans = spectra.shape[0]
    half = TAPS // 2
    index = offsets[:, None] + jnp.arange(chans, dtype=jnp.int32)[None, :]
    beam_t = jnp.transpose(beam_table[index], (2, 1, 0))
    padded = jnp.pad(spectra.astype(jnp.float32), ((half, half), (0, 0), (0, 0)))
    model = jnp.zeros(spectra.shape, jnp.float32)
    for tap in range(TAPS):
        model = model + beam_t[tap][:, :, None] * padded[tap : tap + chans]
    resid = model - observed
    onehot = (kbin[None, :, :] == jnp.arange(KBINS, dtype=jnp.int32)[:, None, None]).astype(
        jnp.float32
    )
    taps_px = jnp.einsum("kt,krc->trc", wedge_taps, onehot, precision=lax.Precision.HIGHEST)
    padded = jnp.pad(resid, ((half, half), (0, 0), (0, 0)))
    wedged = jnp.zeros_like(resid)
    for tap in range(TAPS):
        wedged = wedged + taps_px[tap][None] * padded[tap : tap + chans]
    weighted = inv_variance * wedged
    padded = jnp.pad(weighted, ((half, half), (0, 0), (0, 0)))
    back = jnp.zeros_like(weighted)
    for tap in range(TAPS):
        back = back + taps_px[tap][None] * padded[2 * half - tap : 2 * half - tap + chans]
    back_pad = jnp.pad(back, ((half, half), (0, 0), (0, 0)))
    beam_pad = jnp.pad(beam_t, ((0, 0), (half, half), (0, 0)))
    grad = jnp.zeros_like(back)
    for tap in range(TAPS):
        product = beam_pad[tap][:, :, None] * back_pad
        grad = grad + product[2 * half - tap : 2 * half - tap + chans]
    grad_tiles = lax.all_to_all(
        grad.astype(jnp.bfloat16), "freq", split_axis=0, concat_axis=1, tiled=True
    )
    steps = step_size[:, None, None]
    return field + steps * (score - grad_tiles.astype(jnp.float32)) + jnp.sqrt(2.0 * steps) * noise


def solution(mesh):
    return jax.shard_map(
        per_device,
        mesh=mesh,
        in_specs=(
            P("freq", "skyx", "skyy"),
            P("freq", "skyx", "skyy"),
            P("freq"),
            P(),
            P(),
            P(),
            P(),
            P(None, ("skyx", "freq"), "skyy"),
            P(None, ("skyx", "freq"), "skyy"),
            P(("skyx", "freq")),
            P(),
            P(("skyx", "freq"), "skyy"),
            P(),
        ),
        out_specs=P("freq", "skyx", "skyy"),
        check_vma=False,
    )
```

profile of v0, /device:TPU:0, one launch (start us, length us, event | category | flops | bytes accessed | tf_op | source)
XLA Modules:
  0.0 891.1 jit_solution(10525082798940418208)
XLA Ops:
  1.0 4.9 collective-permute-start
  19.5 12.8 %fusion.9 = bf16[128,64,4,128]{3,1,2,0:T(8,128)(2,1)S(1)} fusion(f32[64]{0:T(128)S(1)} %get-tuple-element.138, f32[128,4,128]{2,1,0:T(4,128)S(1)} %copy.69, f32[64]{0:T(128)S(1)} %get-tuple-element.139, f32[128,4,128]{2,1,0:T(4,128)S(1)} %copy.68, f32[64]{0:T(128)S(1)} %get-tuple-element.132, f32[128,4,128]{2,1,0:T(4,128)S(1)} %copy.67, ...), kind=kLoop, calls=%fused_computation.22 | loop fusion | flops 92274688 | bytes 10750208 | tf_op jit(solution)/shard_map/convert_element_type | solution.py:63
  32.3 3.2 copy-done.2
  38.4 3.7 collective-permute-start.4
  43.4 5.1 all-to-all-start
  49.3 11.8 %fusion.217 = f32[128,4,128,64]{2,3,1,0:T(8,128)} fusion(bf16[128,64,4,128]{3,1,2,0:T(8,128)(2,1)} %copy-done.2, bf16[3,3,64,64]{3,2,1,0:T(8,128)(2,1)S(1)} %copy-done.10), kind=kOutput, calls=%fused_computation.397 | convolution fusion | flops 536870912 | bytes 25182208 | tf_op jit(solution)/shard_map/oc,fchw->fohw/dot_general | solution.py:30
  61.1 24.0 %collective-permute-done.4 = bf16[128,64,1,128]{3,1,2,0:T(8,128)(2,1)S(1)} collective-permute-done((bf16[128,64,1,128]{3,1,2,0:T(8,128)(2,1)}, bf16[128,64,1,128]{3,1,2,0:T(8,128)(2,1)S(1)}, u32[]{:S(2)}, u32[]{:S(2)}) %collective-permute-start.4) | collective-permute-done | bytes 2097184 | tf_op jit(solution)/shard_map/ppermute | solution.py:15
  85.1 4.8 collective-permute-done.5
  89.9 4.2 pad_maximum_fusion.3
  94.1 10.4 %fusion.269 = (bf16[128,64,6,1]{3,1,2,0:T(8,128)(2,1)}, bf16[128,64,6,1]{3,1,2,0:T(8,128)(2,1)}) fusion(bf16[128,64,6,128]{3,1,2,0:T(8,128)(2,1)S(1)} %pad_maximum_fusion.3), kind=kLoop, calls=%fused_computation.493 | loop fusion | bytes 393216 | tf_op jit(solution)/shard_map/slice | solution.py:18
  104.5 16.0 %copy.70 = bf16[128,64,6,1]{0,1,3,2:T(8,128)(2,1)S(1)} copy(bf16[128,64,6,1]{3,1,2,0:T(8,128)(2,1)} %get-tuple-element.78) | data formatting | bytes 196608 | tf_op jit(solution)/shard_map/slice | solution.py:16
  120.5 4.6 collective-permute-start.6
  125.1 16.0 %copy.72 = bf16[128,64,6,1]{0,1,3,2:T(8,128)(2,1)S(1)} copy(bf16[128,64,6,1]{3,1,2,0:T(8,128)(2,1)} %get-tuple-element.77) | data formatting | bytes 196608 | tf_op jit(solution)/shard_map/slice | solution.py:18
  142.7 11.0 %fusion.64 = f32[128,4,128,64]{2,3,1,0:T(8,128)} fusion(bf16[128,64,4,128]{3,1,2,0:T(8,128)(2,1)} %copy-done.2, bf16[128,64,1,128]{3,1,2,0:T(8,128)(2,1)S(1)} %collective-permute-done.4, bf16[3,3,64,64]{3,2,1,0:T(8,128)(2,1)S(1)} %copy-done.10), kind=kOutput, calls=%fused_computation.80 | convolution fusion | flops 553648128 | bytes 27279360 | tf_op jit(solution)/shard_map/oc,fchw->fohw/dot_general | solution.py:30
  153.7 11.6 %fusion.54 = f32[128,4,128,64]{2,3,1,0:T(8,128)} fusion(bf16[128,64,1,128]{3,1,2,0:T(8,128)(2,1)} %collective-permute-done.5, bf16[128,64,4,128]{3,1,2,0:T(8,128)(2,1)} %copy-done.2, bf16[3,3,64,64]{3,2,1,0:T(8,128)(2,1)S(1)} %copy-done.10), kind=kOutput, calls=%fused_computation.69 | convolution fusion | flops 553648128 | bytes 27279360 | tf_op jit(solution)/shard_map/oc,fchw->fohw/dot_general | solution.py:30
  165.2 18.5 %copy.71 = bf16[128,64,6,1]{3,1,2,0:T(8,128)(2,1)} copy(bf16[128,64,6,1]{0,1,3,2:T(8,128)(2,1)S(1)} %collective-permute-done.6) | data formatting | bytes 196608 | tf_op jit(solution)/shard_map/ppermute | solution.py:15
  183.7 18.4 %copy.73 = bf16[128,64,6,1]{3,1,2,0:T(8,128)(2,1)} copy(bf16[128,64,6,1]{0,1,3,2:T(8,128)(2,1)S(1)} %collective-permute-done.7) | data formatting | bytes 196608 | tf_op jit(solution)/shard_map/ppermute | solution.py:18
  202.2 34.7 %pad_maximum_fusion = (bf16[128,64,6,129]{3,1,2,0:T(8,128)(2,1)}, bf16[128,64,6,129]{3,1,2,0:T(8,128)(2,1)}) fusion(bf16[128,64,6,1]{3,1,2,0:T(8,128)(2,1)} %copy.73, bf16[128,64,1,128]{3,1,2,0:T(8,128)(2,1)} %collective-permute-done.5, bf16[128,64,4,128]{3,1,2,0:T(8,128)(2,1)} %copy-done.2, bf16[128,64,1,128]{3,1,2,0:T(8,128)(2,1)S(1)} %collective-permute-done.4, ...), kind=kLoop, calls=%fused_computation.2 | loop fusion | flops 101449728 | bytes 38141952 | tf_op jit(solution)/shard_map/concatenate | solution.py:19
  236.9 11.4 %fusion.56 = f32[128,4,128,64]{2,3,1,0:T(8,128)} fusion(bf16[128,64,6,129]{3,1,2,0:T(8,128)(2,1)} %get-tuple-element.76, bf16[3,3,64,64]{3,2,1,0:T(8,128)(2,1)S(1)} %copy-done.10), kind=kOutput, calls=%fused_computation.71 | convolution fusion | flops 536870912 | bytes 25182208 | tf_op jit(solution)/shard_map/oc,fchw->fohw/dot_general | solution.py:30
  248.3 11.5 %fusion.60 = f32[128,4,128,64]{2,3,1,0:T(8,128)} fusion(bf16[128,64,6,129]{3,1,2,0:T(8,128)(2,1)} %get-tuple-element.76, bf16[3,3,64,64]{3,2,1,0:T(8,128)(2,1)S(1)} %copy-done.10), kind=kOutput, calls=%fused_computation.75 | convolution fusion | flops 536870912 | bytes 25182208 | tf_op jit(solution)/shard_map/oc,fchw->fohw/dot_general | solution.py:30
  259.8 14.4 %fusion.58 = f32[128,4,128,64]{2,3,1,0:T(8,128)} fusion(bf16[128,64,6,129]{3,1,2,0:T(8,128)(2,1)} %get-tuple-element.75, bf16[3,3,64,64]{3,2,1,0:T(8,128)(2,1)S(1)} %copy-done.10), kind=kOutput, calls=%fused_computation.73 | convolution fusion | flops 536870912 | bytes 25182208 | tf_op jit(solution)/shard_map/oc,fchw->fohw/dot_general | solution.py:30
  274.3 14.4 %fusion.62 = f32[128,4,128,64]{2,3,1,0:T(8,128)} fusion(bf16[128,64,6,129]{3,1,2,0:T(8,128)(2,1)} %get-tuple-element.75, bf16[3,3,64,64]{3,2,1,0:T(8,128)(2,1)S(1)} %copy-done.10), kind=kOutput, calls=%fused_computation.77 | convolution fusion | flops 536870912 | bytes 25182208 | tf_op jit(solution)/shard_map/oc,fchw->fohw/dot_general | solution.py:30
  288.7 11.7 %fusion.66 = f32[128,4,128,64]{2,3,1,0:T(8,128)} fusion(bf16[128,64,6,129]{3,1,2,0:T(8,128)(2,1)} %get-tuple-element.76, bf16[3,3,64,64]{3,2,1,0:T(8,128)(2,1)S(1)} %copy-done.10), kind=kOutput, calls=%fused_computation.82 | convolution fusion | flops 536870912 | bytes 25182208 | tf_op jit(solution)/shard_map/oc,fchw->fohw/dot_general | solution.py:30
  300.4 51.3 %fusion.10 = bf16[128,64,4,128]{3,1,2,0:T(8,128)(2,1)} fusion(f32[128,4,128,64]{2,3,1,0:T(8,128)} %fusion.54, f32[128,4,128,64]{2,3,1,0:T(8,128)} %fusion.56, f32[128,4,128,64]{2,3,1,0:T(8,128)} %fusion.58, f32[128,4,128,64]{2,3,1,0:T(8,128)} %fusion.217, f32[128,4,128,64]{2,3,1,0:T(8,128)} %fusion.60, f32[128,4,128,64]{2,3,1,0:T(8,128)} %fusion.62, ...), kind=kOutput, calls=%fused_computation.23 | convolution fusion | flops 591396864 | bytes 151011328 | tf_op jit(solution)/shard_map/oc,fchw->fohw/dot_general | solution.py:30
  351.7 5.2 fusion.271
  361.3 3.5 slice_reduce_fusion.30
  371.9 11.6 %fusion.207 = f32[128,4,128,64]{2,3,1,0:T(8,128)} fusion(bf16[128,64,4,128]{3,1,2,0:T(8,128)(2,1)} %fusion.10, bf16[3,3,64,64]{3,2,1,0:T(8,128)(2,1)S(1)} %copy-done.11), kind=kOutput, calls=%fused_computation.387 | convolution fusion | flops 536870912 | bytes 25182208 | tf_op jit(solution)/shard_map/oc,fchw->fohw/dot_general | solution.py:30
  383.4 21.3 %collective-permute-done.8 = bf16[128,64,1,128]{3,1,2,0:T(8,128)(2,1)S(1)} collective-permute-done((bf16[128,64,1,128]{3,1,2,0:T(8,128)(2,1)}, bf16[128,64,1,128]{3,1,2,0:T(8,128)(2,1)S(1)}, u32[]{:S(2)}, u32[]{:S(2)}) %collective-permute-start.8) | collective-permute-done | bytes 2097184 | tf_op jit(solution)/shard_map/ppermute | solution.py:15
  404.7 4.6 collective-permute-done.9
  409.3 4.2 pad_maximum_fusion.4
  413.5 10.4 %fusion.268 = (bf16[128,64,6,1]{3,1,2,0:T(8,128)(2,1)}, bf16[128,64,6,1]{3,1,2,0:T(8,128)(2,1)}) fusion(bf16[128,64,6,128]{3,1,2,0:T(8,128)(2,1)S(1)} %pad_maximum_fusion.4), kind=kLoop, calls=%fused_computation.492 | loop fusion | bytes 393216 | tf_op jit(solution)/shard_map/slice | solution.py:18
  423.9 16.0 %copy.74 = bf16[128,64,6,1]{0,1,3,2:T(8,128)(2,1)S(1)} copy(bf16[128,64,6,1]{3,1,2,0:T(8,128)(2,1)} %get-tuple-element.74) | data formatting | bytes 196608 | tf_op jit(solution)/shard_map/slice | solution.py:16
  441.8 16.5 %copy.76 = bf16[128,64,6,1]{0,1,3,2:T(8,128)(2,1)S(1)} copy(bf16[128,64,6,1]{3,1,2,0:T(8,128)(2,1)} %get-tuple-element.73) | data formatting | bytes 196608 | tf_op jit(solution)/shard_map/slice | solution.py:18
  459.6 11.0 %fusion.46 = f32[128,4,128,64]{2,3,1,0:T(8,128)} fusion(bf16[128,64,4,128]{3,1,2,0:T(8,128)(2,1)} %fusion.10, bf16[128,64,1,128]{3,1,2,0:T(8,128)(2,1)S(1)} %collective-permute-done.8, bf16[3,3,64,64]{3,2,1,0:T(8,128)(2,1)S(1)} %copy-done.11), kind=kOutput, calls=%fused_computation.62 | convolution fusion | flops 553648128 | bytes 27279360 | tf_op jit(solution)/shard_map/oc,fchw->fohw/dot_general | solution.py:30
  470.5 11.6 %fusion.36 = f32[128,4,128,64]{2,3,1,0:T(8,128)} fusion(bf16[128,64,1,128]{3,1,2,0:T(8,128)(2,1)} %collective-permute-done.9, bf16[128,64,4,128]{3,1,2,0:T(8,128)(2,1)} %fusion.10, bf16[3,3,64,64]{3,2,1,0:T(8,128)(2,1)S(1)} %copy-done.11), kind=kOutput, calls=%fused_computation.51 | convolution fusion | flops 553648128 | bytes 27279360 | tf_op jit(solution)/shard_map/oc,fchw->fohw/dot_general | solution.py:30
  482.1 18.5 %copy.75 = bf16[128,64,6,1]{3,1,2,0:T(8,128)(2,1)} copy(bf16[128,64,6,1]{0,1,3,2:T(8,128)(2,1)S(1)} %collective-permute-done.10) | data formatting | bytes 196608 | tf_op jit(solution)/shard_map/ppermute | solution.py:15
  500.6 18.4 %copy.77 = bf16[128,64,6,1]{3,1,2,0:T(8,128)(2,1)} copy(bf16[128,64,6,1]{0,1,3,2:T(8,128)(2,1)S(1)} %collective-permute-done.11) | data formatting | bytes 196608 | tf_op jit(solution)/shard_map/ppermute | solution.py:18
  519.0 34.3 %pad_maximum_fusion.1 = (bf16[128,64,6,129]{3,1,2,0:T(8,128)(2,1)}, bf16[128,64,6,129]{3,1,2,0:T(8,128)(2,1)}) fusion(bf16[128,64,6,1]{3,1,2,0:T(8,128)(2,1)} %copy.77, bf16[128,64,1,128]{3,1,2,0:T(8,128)(2,1)} %collective-permute-done.9, bf16[128,64,4,128]{3,1,2,0:T(8,128)(2,1)} %fusion.10, bf16[128,64,1,128]{3,1,2,0:T(8,128)(2,1)S(1)} %collective-permute-done.8, ...), kind=kLoop, calls=%fused_computation.4 | loop fusion | flops 101449728 | bytes 38141952 | tf_op jit(solution)/shard_map/concatenate | solution.py:19
  553.3 11.4 %fusion.38 = f32[128,4,128,64]{2,3,1,0:T(8,128)} fusion(bf16[128,64,6,129]{3,1,2,0:T(8,128)(2,1)} %get-tuple-element.72, bf16[3,3,64,64]{3,2,1,0:T(8,128)(2,1)S(1)} %copy-done.11), kind=kOutput, calls=%fused_computation.53 | convolution fusion | flops 536870912 | bytes 25182208 | tf_op jit(solution)/shard_map/oc,fchw->fohw/dot_general | solution.py:30
  564.7 11.5 %fusion.42 = f32[128,4,128,64]{2,3,1,0:T(8,128)} fusion(bf16[128,64,6,129]{3,1,2,0:T(8,128)(2,1)} %get-tuple-element.72, bf16[3,3,64,64]{3,2,1,0:T(8,128)(2,1)S(1)} %copy-done.11), kind=kOutput, calls=%fused_computation.57 | convolution fusion | flops 536870912 | bytes 25182208 | tf_op jit(solution)/shard_map/oc,fchw->fohw/dot_general | solution.py:30
  576.3 14.4 %fusion.40 = f32[128,4,128,64]{2,3,1,0:T(8,128)} fusion(bf16[128,64,6,129]{3,1,2,0:T(8,128)(2,1)} %get-tuple-element.71, bf16[3,3,64,64]{3,2,1,0:T(8,128)(2,1)S(1)} %copy-done.11), kind=kOutput, calls=%fused_computation.55 | convolution fusion | flops 536870912 | bytes 25182208 | tf_op jit(solution)/shard_map/oc,fchw->fohw/dot_general | solution.py:30
  590.7 14.4 %fusion.44 = f32[128,4,128,64]{2,3,1,0:T(8,128)} fusion(bf16[128,64,6,129]{3,1,2,0:T(8,128)(2,1)} %get-tuple-element.71, bf16[3,3,64,64]{3,2,1,0:T(8,128)(2,1)S(1)} %copy-done.11), kind=kOutput, calls=%fused_computation.59 | convolution fusion | flops 536870912 | bytes 25182208 | tf_op jit(solution)/shard_map/oc,fchw->fohw/dot_general | solution.py:30
  605.1 11.7 %fusion.48 = f32[128,4,128,64]{2,3,1,0:T(8,128)} fusion(bf16[128,64,6,129]{3,1,2,0:T(8,128)(2,1)} %get-tuple-element.72, bf16[3,3,64,64]{3,2,1,0:T(8,128)(2,1)S(1)} %copy-done.11), kind=kOutput, calls=%fused_computation.64 | convolution fusion | flops 536870912 | bytes 25182208 | tf_op jit(solution)/shard_map/oc,fchw->fohw/dot_general | solution.py:30
  617.2 51.3 %fusion.11 = bf16[128,64,4,128]{3,1,2,0:T(8,128)(2,1)} fusion(f32[128,4,128,64]{2,3,1,0:T(8,128)} %fusion.36, f32[128,4,128,64]{2,3,1,0:T(8,128)} %fusion.38, f32[128,4,128,64]{2,3,1,0:T(8,128)} %fusion.40, f32[128,4,128,64]{2,3,1,0:T(8,128)} %fusion.207, f32[128,4,128,64]{2,3,1,0:T(8,128)} %fusion.42, f32[128,4,128,64]{2,3,1,0:T(8,128)} %fusion.44, ...), kind=kOutput, calls=%fused_computation.24 | convolution fusion | flops 591396864 | bytes 151011328 | tf_op jit(solution)/shard_map/oc,fchw->fohw/dot_general | solution.py:30
  668.5 5.1 fusion.270
  681.8 3.5 add_subtract_fusion
  692.9 5.3 all-to-all-start.1
  698.8 5.9 all-to-all-done.1
  704.9 4.7 fusion.246
  709.6 11.5 %collective-permute-done.12 = bf16[128,64,1,128]{3,1,2,0:T(8,128)(2,1)S(1)} collective-permute-done((bf16[128,64,1,128]{3,1,2,0:T(8,128)(2,1)}, bf16[128,64,1,128]{3,1,2,0:T(8,128)(2,1)S(1)}, u32[]{:S(2)}, u32[]{:S(2)}) %collective-permute-start.12) | collective-permute-done | bytes 2097184 | tf_op jit(solution)/shard_map/ppermute | solution.py:15
  721.1 4.8 collective-permute-done.13
  725.9 4.2 pad_maximum_fusion.5
  730.1 10.4 %fusion.267 = (bf16[128,64,6,1]{3,1,2,0:T(8,128)(2,1)}, bf16[128,64,6,1]{3,1,2,0:T(8,128)(2,1)}) fusion(bf16[128,64,6,128]{3,1,2,0:T(8,128)(2,1)S(1)} %pad_maximum_fusion.5), kind=kLoop, calls=%fused_computation.491 | loop fusion | bytes 393216 | tf_op jit(solution)/shard_map/slice | solution.py:16
  740.5 16.0 %copy.78 = bf16[128,64,6,1]{0,1,3,2:T(8,128)(2,1)S(1)} copy(bf16[128,64,6,1]{3,1,2,0:T(8,128)(2,1)} %get-tuple-element.69) | data formatting | bytes 196608 | tf_op jit(solution)/shard_map/slice | solution.py:16
  758.6 16.0 %copy.80 = bf16[128,64,6,1]{0,1,3,2:T(8,128)(2,1)S(1)} copy(bf16[128,64,6,1]{3,1,2,0:T(8,128)(2,1)} %get-tuple-element.70) | data formatting | bytes 196608 | tf_op jit(solution)/shard_map/slice | solution.py:18
  775.9 4.1 fusion.12
  780.0 4.6 fusion.16
  784.6 18.5 %copy.79 = bf16[128,64,6,1]{3,1,2,0:T(8,128)(2,1)} copy(bf16[128,64,6,1]{0,1,3,2:T(8,128)(2,1)S(1)} %collective-permute-done.14) | data formatting | bytes 196608 | tf_op jit(solution)/shard_map/ppermute | solution.py:15
  803.1 18.5 %copy.81 = bf16[128,64,6,1]{3,1,2,0:T(8,128)(2,1)} copy(bf16[128,64,6,1]{0,1,3,2:T(8,128)(2,1)S(1)} %collective-permute-done.15) | data formatting | bytes 196608 | tf_op jit(solution)/shard_map/ppermute | solution.py:18
  821.6 34.4 %maximum_maximum_fusion.2 = (bf16[128,64,6,129]{3,1,2,0:T(8,128)(2,1)}, bf16[128,64,6,129]{3,1,2,0:T(8,128)(2,1)}) fusion(bf16[128,64,1,128]{3,1,2,0:T(8,128)(2,1)} %collective-permute-done.13, bf16[128,64,4,128]{3,1,2,0:T(8,128)(2,1)} %fusion.11, bf16[128,64,1,128]{3,1,2,0:T(8,128)(2,1)S(1)} %collective-permute-done.12, bf16[128,64,6,1]{3,1,2,0:T(8,128)(2,1)} %copy.79, ...), kind=kLoop, calls=%fused_computation.5 | loop fusion | flops 101449728 | bytes 38141952 | tf_op jit(solution)/shard_map/concatenate | solution.py:19
  855.9 8.8 fusion.20
  864.7 9.4 %fusion.24 = f32[1,128,4,128]{3,0,2,1:T(1,128)S(1)} fusion(bf16[128,64,6,129]{3,1,2,0:T(8,128)(2,1)} %get-tuple-element.68, bf16[3,3,1,64]{3,1,2,0:T(4,128)(2,1)S(1)} %copy-done.51), kind=kOutput, calls=%fused_computation.40 | convolution fusion | flops 8388608 | bytes 8651264 | tf_op jit(solution)/shard_map/oc,fchw->fohw/dot_general | solution.py:30
  874.1 4.6 fusion.22
  880.0 8.6 fusion.28
  (220 shorter events, 58.0 us)
Async XLA Ops:
  0.0 370.4 %copy-start = (f32[8,31]{1,0:T(8,128)S(1)}, f32[8,31]{1,0:T(8,128)}, u32[]{:S(2)}) copy-start(f32[8,31]{1,0:T(8,128)} %param.25) | copy-start | bytes 2980
  0.0 49.3 %copy-start.10 = (bf16[3,3,64,64]{3,2,1,0:T(8,128)(2,1)S(1)}, bf16[3,3,64,64]{3,2,1,0:T(8,128)(2,1)}, u32[]{:S(2)}) copy-start(bf16[3,3,64,64]{3,2,1,0:T(8,128)(2,1)} %param.17) | copy-start | bytes 221188
  1.0 9.7 %collective-permute-start = (bf16[128,1,1,128]{3,0,2,1:T(8,128)(2,1)S(1)}, bf16[128,1,1,128]{3,0,2,1:T(8,128)(2,1)S(1)}, u32[]{:S(2)}, u32[]{:S(2)}) collective-permute-start(bf16[128,1,1,128]{3,0,2,1:T(8,128)(2,1)S(1)} %get-tuple-element.98), channel_id=1, source_target_pairs={{0,16},{1,17},{2,18},{3,19},{4,20},{5,21},{6,22},{7,23},{8,24},{9,... | collective-permute-start | bytes 98312 | tf_op jit(solution)/shard_map/ppermute | solution.py:15
  5.9 5.8 collective-permute-start.1
  11.9 3.2 collective-permute-start.2
  13.2 5.1 collective-permute-start.3
  38.4 46.7 %collective-permute-start.4 = (bf16[128,64,1,128]{3,1,2,0:T(8,128)(2,1)}, bf16[128,64,1,128]{3,1,2,0:T(8,128)(2,1)S(1)}, u32[]{:S(2)}, u32[]{:S(2)}) collective-permute-start(bf16[128,64,1,128]{3,1,2,0:T(8,128)(2,1)} %get-tuple-element.83), channel_id=1, source_target_pairs={{0,16},{1,17},{2,18},{3,19},{4,20},{5,21},{6,22},{7,23},{8,24},{9,... | collective-permute-start | bytes 6291464 | tf_op jit(solution)/shard_map/ppermute | solution.py:15
  42.1 47.8 %collective-permute-start.5 = (bf16[128,64,1,128]{3,1,2,0:T(8,128)(2,1)}, bf16[128,64,1,128]{3,1,2,0:T(8,128)(2,1)}, u32[]{:S(2)}, u32[]{:S(2)}) collective-permute-start(bf16[128,64,1,128]{3,1,2,0:T(8,128)(2,1)} %get-tuple-element.84), channel_id=1, source_target_pairs={{16,0},{17,1},{18,2},{19,3},{20,4},{21,5},{22,6},{23,7},{24,8},{25... | collective-permute-start | bytes 6291464 | tf_op jit(solution)/shard_map/ppermute | solution.py:18
  43.4 637.3 %all-to-all-start = ((bf16[128,4,128]{2,0,1:T(8,128)(2,1)}), bf16[128,4,128]{2,0,1:T(8,128)(2,1)}, u32[]{:S(2)}, u32[]{:S(2)}) async-start(bf16[128,4,128]{2,0,1:T(8,128)(2,1)} %copy.140), calls=%async_computation | async-start | bytes 262144 | tf_op jit(solution)/shard_map/all_to_all | solution.py:65
  48.4 41.4 %slice-start.2 = ((s8[8388608]{0:T(1024)(128)(4,1)}), s8[4194304]{0:T(1024)(128)(4,1)S(1)}, s32[]{:S(2)}) async-start(s8[8388608]{0:T(1024)(128)(4,1)} %bitcast.434), calls=%async_computation.4 | async-start | bytes 8388608
  49.3 40.6 %slice-start.3 = ((s8[8388608]{0:T(1024)(128)(4,1)}), s8[4194304]{0:T(1024)(128)(4,1)S(1)}, s32[]{:S(2)}) async-start(s8[8388608]{0:T(1024)(128)(4,1)} %bitcast.434), calls=%async_computation.5 | async-start | bytes 8388608
  120.5 44.7 %collective-permute-start.6 = (bf16[128,64,6,1]{0,1,3,2:T(8,128)(2,1)S(1)}, bf16[128,64,6,1]{0,1,3,2:T(8,128)(2,1)S(1)}, u32[]{:S(2)}, u32[]{:S(2)}) collective-permute-start(bf16[128,64,6,1]{0,1,3,2:T(8,128)(2,1)S(1)} %copy.70), channel_id=1, source_target_pairs={{0,4},{4,8},{8,12},{1,5},{5,9},{9,13},{2,6},{6,10},{10,14},{3,7},{... | collective-permute-start | bytes 294920 | tf_op jit(solution)/shard_map/ppermute | solution.py:15
  141.2 42.5 %collective-permute-start.7 = (bf16[128,64,6,1]{0,1,3,2:T(8,128)(2,1)S(1)}, bf16[128,64,6,1]{0,1,3,2:T(8,128)(2,1)S(1)}, u32[]{:S(2)}, u32[]{:S(2)}) collective-permute-start(bf16[128,64,6,1]{0,1,3,2:T(8,128)(2,1)S(1)} %copy.72), channel_id=1, source_target_pairs={{4,0},{8,4},{12,8},{5,1},{9,5},{13,9},{6,2},{10,6},{14,10},{7,3},{... | collective-permute-start | bytes 294920 | tf_op jit(solution)/shard_map/ppermute | solution.py:18
  300.4 59.6 %copy-start.12 = (f32[1024,31]{0,1:T(8,128)S(1)}, f32[1024,31]{0,1:T(8,128)}, u32[]{:S(2)}) copy-start(f32[1024,31]{0,1:T(8,128)} %param.23) | copy-start | bytes 380932
  356.8 47.9 %collective-permute-start.8 = (bf16[128,64,1,128]{3,1,2,0:T(8,128)(2,1)}, bf16[128,64,1,128]{3,1,2,0:T(8,128)(2,1)S(1)}, u32[]{:S(2)}, u32[]{:S(2)}) collective-permute-start(bf16[128,64,1,128]{3,1,2,0:T(8,128)(2,1)} %get-tuple-element.81), channel_id=1, source_target_pairs={{0,16},{1,17},{2,18},{3,19},{4,20},{5,21},{6,22},{7,23},{8,24},{9,... | collective-permute-start | bytes 6291464 | tf_op jit(solution)/shard_map/ppermute | solution.py:15
  358.7 50.6 %collective-permute-start.9 = (bf16[128,64,1,128]{3,1,2,0:T(8,128)(2,1)}, bf16[128,64,1,128]{3,1,2,0:T(8,128)(2,1)}, u32[]{:S(2)}, u32[]{:S(2)}) collective-permute-start(bf16[128,64,1,128]{3,1,2,0:T(8,128)(2,1)} %get-tuple-element.82), channel_id=1, source_target_pairs={{16,0},{17,1},{18,2},{19,3},{20,4},{21,5},{22,6},{23,7},{24,8},{25... | collective-permute-start | bytes 6291464 | tf_op jit(solution)/shard_map/ppermute | solution.py:18
  364.9 44.4 %slice-start = ((s8[8388608]{0:T(1024)(128)(4,1)}), s8[4194304]{0:T(1024)(128)(4,1)S(1)}, s32[]{:S(2)}) async-start(s8[8388608]{0:T(1024)(128)(4,1)} %bitcast.432), calls=%async_computation.2 | async-start | bytes 8388608
  439.9 42.2 %collective-permute-start.10 = (bf16[128,64,6,1]{0,1,3,2:T(8,128)(2,1)S(1)}, bf16[128,64,6,1]{0,1,3,2:T(8,128)(2,1)S(1)}, u32[]{:S(2)}, u32[]{:S(2)}) collective-permute-start(bf16[128,64,6,1]{0,1,3,2:T(8,128)(2,1)S(1)} %copy.74), channel_id=1, source_target_pairs={{0,4},{4,8},{8,12},{1,5},{5,9},{9,13},{2,6},{6,10},{10,14},{3,7},{... | collective-permute-start | bytes 294920 | tf_op jit(solution)/shard_map/ppermute | solution.py:15
  458.3 42.3 %collective-permute-start.11 = (bf16[128,64,6,1]{0,1,3,2:T(8,128)(2,1)S(1)}, bf16[128,64,6,1]{0,1,3,2:T(8,128)(2,1)S(1)}, u32[]{:S(2)}, u32[]{:S(2)}) collective-permute-start(bf16[128,64,6,1]{0,1,3,2:T(8,128)(2,1)S(1)} %copy.76), channel_id=1, source_target_pairs={{4,0},{8,4},{12,8},{5,1},{9,5},{13,9},{6,2},{10,6},{14,10},{7,3},{... | collective-permute-start | bytes 294920 | tf_op jit(solution)/shard_map/ppermute | solution.py:18
  616.8 59.7 %copy-start.4 = (f32[512,31]{1,0:T(8,128)S(1)}, f32[512,31]{1,0:T(8,128)}, u32[]{:S(2)}) copy-start(f32[512,31]{1,0:T(8,128)} %copy-done.3) | copy-start | bytes 190468
  616.8 61.6 %copy-start.31 = (f32[542]{0:T(1024)S(1)}, f32[542]{0:T(1024)}, u32[]{:S(2)}) copy-start(f32[542]{0:T(1024)} %get-tuple-element.5) | copy-start | bytes 6508
  616.9 61.7 %copy-start.30 = (f32[542]{0:T(1024)S(1)}, f32[542]{0:T(1024)}, u32[]{:S(2)}) copy-start(f32[542]{0:T(1024)} %get-tuple-element.6) | copy-start | bytes 6508
  616.9 61.8 %copy-start.29 = (f32[542]{0:T(1024)S(1)}, f32[542]{0:T(1024)}, u32[]{:S(2)}) copy-start(f32[542]{0:T(1024)} %get-tuple-element.7) | copy-start | bytes 6508
  616.9 61.8 %copy-start.28 = (f32[542]{0:T(1024)S(1)}, f32[542]{0:T(1024)}, u32[]{:S(2)}) copy-start(f32[542]{0:T(1024)} %get-tuple-element.8) | copy-start | bytes 6508
  616.9 61.9 %copy-start.27 = (f32[542]{0:T(1024)S(1)}, f32[542]{0:T(1024)}, u32[]{:S(2)}) copy-start(f32[542]{0:T(1024)} %get-tuple-element.9) | copy-start | bytes 6508
  616.9 62.0 %copy-start.26 = (f32[542]{0:T(1024)S(1)}, f32[542]{0:T(1024)}, u32[]{:S(2)}) copy-start(f32[542]{0:T(1024)} %get-tuple-element.10) | copy-start | bytes 6508
  616.9 62.0 %copy-start.25 = (f32[542]{0:T(1024)S(1)}, f32[542]{0:T(1024)}, u32[]{:S(2)}) copy-start(f32[542]{0:T(1024)} %get-tuple-element.11) | copy-start | bytes 6508
  616.9 62.1 %copy-start.24 = (f32[542]{0:T(1024)S(1)}, f32[542]{0:T(1024)}, u32[]{:S(2)}) copy-start(f32[542]{0:T(1024)} %get-tuple-element.12) | copy-start | bytes 6508
  616.9 62.1 %copy-start.23 = (f32[542]{0:T(1024)S(1)}, f32[542]{0:T(1024)}, u32[]{:S(2)}) copy-start(f32[542]{0:T(1024)} %get-tuple-element.13) | copy-start | bytes 6508
  616.9 62.2 %copy-start.22 = (f32[542]{0:T(1024)S(1)}, f32[542]{0:T(1024)}, u32[]{:S(2)}) copy-start(f32[542]{0:T(1024)} %get-tuple-element.14) | copy-start | bytes 6508
  616.9 62.3 %copy-start.21 = (f32[542]{0:T(1024)S(1)}, f32[542]{0:T(1024)}, u32[]{:S(2)}) copy-start(f32[542]{0:T(1024)} %get-tuple-element.15) | copy-start | bytes 6508
  616.9 62.3 %copy-start.20 = (f32[542]{0:T(1024)S(1)}, f32[542]{0:T(1024)}, u32[]{:S(2)}) copy-start(f32[542]{0:T(1024)} %get-tuple-element.16) | copy-start | bytes 6508
  616.9 62.4 %copy-start.19 = (f32[542]{0:T(1024)S(1)}, f32[542]{0:T(1024)}, u32[]{:S(2)}) copy-start(f32[542]{0:T(1024)} %get-tuple-element.17) | copy-start | bytes 6508
  617.0 62.5 %copy-start.18 = (f32[542]{0:T(1024)S(1)}, f32[542]{0:T(1024)}, u32[]{:S(2)}) copy-start(f32[542]{0:T(1024)} %get-tuple-element.18) | copy-start | bytes 6508
  617.0 62.5 %copy-start.17 = (f32[542]{0:T(1024)S(1)}, f32[542]{0:T(1024)}, u32[]{:S(2)}) copy-start(f32[542]{0:T(1024)} %get-tuple-element.19) | copy-start | bytes 6508
  617.0 62.6 %copy-start.16 = (f32[542]{0:T(1024)S(1)}, f32[542]{0:T(1024)}, u32[]{:S(2)}) copy-start(f32[542]{0:T(1024)} %get-tuple-element.20) | copy-start | bytes 6508
  617.0 62.7 %copy-start.15 = (f32[542]{0:T(1024)S(1)}, f32[542]{0:T(1024)}, u32[]{:S(2)}) copy-start(f32[542]{0:T(1024)} %get-tuple-element.21) | copy-start | bytes 6508
  617.0 62.7 %copy-start.14 = (f32[542]{0:T(1024)S(1)}, f32[542]{0:T(1024)}, u32[]{:S(2)}) copy-start(f32[542]{0:T(1024)} %get-tuple-element.22) | copy-start | bytes 6508
  617.0 62.8 %copy-start.13 = (f32[542]{0:T(1024)S(1)}, f32[542]{0:T(1024)}, u32[]{:S(2)}) copy-start(f32[542]{0:T(1024)} %get-tuple-element.23) | copy-start | bytes 6508
  617.0 64.6 %copy-start.7 = (f32[512,1,128]{2,1,0:T(1,128)S(1)}, f32[512,1,128]{2,1,0:T(1,128)}, u32[]{:S(2)}) copy-start(f32[512,1,128]{2,1,0:T(1,128)} %param.20) | copy-start | bytes 786436
  617.0 64.6 %copy-start.32 = (f32[512]{0:T(512)S(1)}, f32[512]{0:T(512)}, u32[]{:S(2)}) copy-start(f32[512]{0:T(512)} %get-tuple-element.55) | copy-start | bytes 6148
  617.0 64.6 %copy-start.33 = (f32[512]{0:T(512)S(1)}, f32[512]{0:T(512)}, u32[]{:S(2)}) copy-start(f32[512]{0:T(512)} %get-tuple-element.56) | copy-start | bytes 6148
  617.1 64.6 %copy-start.34 = (f32[512]{0:T(512)S(1)}, f32[512]{0:T(512)}, u32[]{:S(2)}) copy-start(f32[512]{0:T(512)} %get-tuple-element.57) | copy-start | bytes 6148
  617.1 64.6 %copy-start.35 = (f32[512]{0:T(512)S(1)}, f32[512]{0:T(512)}, u32[]{:S(2)}) copy-start(f32[512]{0:T(512)} %get-tuple-element.58) | copy-start | bytes 6148
  617.1 64.6 %copy-start.36 = (f32[512]{0:T(512)S(1)}, f32[512]{0:T(512)}, u32[]{:S(2)}) copy-start(f32[512]{0:T(512)} %get-tuple-element.59) | copy-start | bytes 6148
  617.1 64.6 %copy-start.37 = (f32[512]{0:T(512)S(1)}, f32[512]{0:T(512)}, u32[]{:S(2)}) copy-start(f32[512]{0:T(512)} %get-tuple-element.60) | copy-start | bytes 6148
  617.1 64.6 %copy-start.38 = (f32[512]{0:T(512)S(1)}, f32[512]{0:T(512)}, u32[]{:S(2)}) copy-start(f32[512]{0:T(512)} %get-tuple-element.61) | copy-start | bytes 6148
  617.1 64.6 %copy-start.39 = (f32[512]{0:T(512)S(1)}, f32[512]{0:T(512)}, u32[]{:S(2)}) copy-start(f32[512]{0:T(512)} %get-tuple-element.62) | copy-start | bytes 6148
  617.1 64.6 %copy-start.40 = (f32[512]{0:T(512)S(1)}, f32[512]{0:T(512)}, u32[]{:S(2)}) copy-start(f32[512]{0:T(512)} %get-tuple-element.63) | copy-start | bytes 6148
  617.1 64.6 %copy-start.41 = (f32[512]{0:T(512)S(1)}, f32[512]{0:T(512)}, u32[]{:S(2)}) copy-start(f32[512]{0:T(512)} %get-tuple-element.64) | copy-start | bytes 6148
  617.1 64.6 %copy-start.42 = (f32[512]{0:T(512)S(1)}, f32[512]{0:T(512)}, u32[]{:S(2)}) copy-start(f32[512]{0:T(512)} %get-tuple-element.65) | copy-start | bytes 6148
  617.1 64.6 %copy-start.43 = (f32[512]{0:T(512)S(1)}, f32[512]{0:T(512)}, u32[]{:S(2)}) copy-start(f32[512]{0:T(512)} %get-tuple-element.66) | copy-start | bytes 6148
  617.2 64.6 %copy-start.44 = (f32[512]{0:T(512)S(1)}, f32[512]{0:T(512)}, u32[]{:S(2)}) copy-start(f32[512]{0:T(512)} %get-tuple-element.36) | copy-start | bytes 6148
  617.2 64.6 %copy-start.45 = (f32[512]{0:T(512)S(1)}, f32[512]{0:T(512)}, u32[]{:S(2)}) copy-start(f32[512]{0:T(512)} %get-tuple-element.37) | copy-start | bytes 6148
  617.2 64.6 %copy-start.46 = (f32[512]{0:T(512)S(1)}, f32[512]{0:T(512)}, u32[]{:S(2)}) copy-start(f32[512]{0:T(512)} %get-tuple-element.38) | copy-start | bytes 6148
  617.2 64.6 %copy-start.47 = (f32[512]{0:T(512)S(1)}, f32[512]{0:T(512)}, u32[]{:S(2)}) copy-start(f32[512]{0:T(512)} %get-tuple-element.39) | copy-start | bytes 6148
  617.2 64.6 %copy-start.48 = (f32[512]{0:T(512)S(1)}, f32[512]{0:T(512)}, u32[]{:S(2)}) copy-start(f32[512]{0:T(512)} %get-tuple-element.40) | copy-start | bytes 6148
  617.2 64.6 %copy-start.49 = (f32[512]{0:T(512)S(1)}, f32[512]{0:T(512)}, u32[]{:S(2)}) copy-start(f32[512]{0:T(512)} %get-tuple-element.41) | copy-start | bytes 6148
  617.2 68.1 %copy-start.9 = (f32[512,1,128]{2,1,0:T(1,128)S(1)}, f32[512,1,128]{2,1,0:T(1,128)}, u32[]{:S(2)}) copy-start(f32[512,1,128]{2,1,0:T(1,128)} %param.21) | copy-start | bytes 786436
  673.6 47.5 %collective-permute-start.12 = (bf16[128,64,1,128]{3,1,2,0:T(8,128)(2,1)}, bf16[128,64,1,128]{3,1,2,0:T(8,128)(2,1)S(1)}, u32[]{:S(2)}, u32[]{:S(2)}) collective-permute-start(bf16[128,64,1,128]{3,1,2,0:T(8,128)(2,1)} %get-tuple-element.79), channel_id=1, source_target_pairs={{0,16},{1,17},{2,18},{3,19},{4,20},{5,21},{6,22},{7,23},{8,24},{9,... | collective-permute-start | bytes 6291464 | tf_op jit(solution)/shard_map/ppermute | solution.py:15
  675.2 50.7 %collective-permute-start.13 = (bf16[128,64,1,128]{3,1,2,0:T(8,128)(2,1)}, bf16[128,64,1,128]{3,1,2,0:T(8,128)(2,1)}, u32[]{:S(2)}, u32[]{:S(2)}) collective-permute-start(bf16[128,64,1,128]{3,1,2,0:T(8,128)(2,1)} %get-tuple-element.80), channel_id=1, source_target_pairs={{16,0},{17,1},{18,2},{19,3},{20,4},{21,5},{22,6},{23,7},{24,8},{25... | collective-permute-start | bytes 6291464 | tf_op jit(solution)/shard_map/ppermute | solution.py:18
  692.9 11.8 %all-to-all-start.1 = ((bf16[4,2,8192]{2,1,0:T(2,128)(2,1)}), bf16[4,2,8192]{2,1,0:T(2,128)(2,1)S(1)}, u32[]{:S(2)}, u32[]{:S(2)}) async-start(bf16[4,2,8192]{2,1,0:T(2,128)(2,1)} %reshape.723), calls=%async_computation.1 | async-start | bytes 262144 | tf_op jit(solution)/shard_map/all_to_all | solution.py:94
  756.5 28.1 %collective-permute-start.14 = (bf16[128,64,6,1]{0,1,3,2:T(8,128)(2,1)S(1)}, bf16[128,64,6,1]{0,1,3,2:T(8,128)(2,1)S(1)}, u32[]{:S(2)}, u32[]{:S(2)}) collective-permute-start(bf16[128,64,6,1]{0,1,3,2:T(8,128)(2,1)S(1)} %copy.78), channel_id=1, source_target_pairs={{0,4},{4,8},{8,12},{1,5},{5,9},{9,13},{2,6},{6,10},{10,14},{3,7},{... | collective-permute-start | bytes 294920 | tf_op jit(solution)/shard_map/ppermute | solution.py:15
  774.6 28.5 %collective-permute-start.15 = (bf16[128,64,6,1]{0,1,3,2:T(8,128)(2,1)S(1)}, bf16[128,64,6,1]{0,1,3,2:T(8,128)(2,1)S(1)}, u32[]{:S(2)}, u32[]{:S(2)}) collective-permute-start(bf16[128,64,6,1]{0,1,3,2:T(8,128)(2,1)S(1)} %copy.80), channel_id=1, source_target_pairs={{4,0},{8,4},{12,8},{5,1},{9,5},{13,9},{6,2},{10,6},{14,10},{7,3},{... | collective-permute-start | bytes 294920 | tf_op jit(solution)/shard_map/ppermute | solution.py:18
  (13 other events, 251.9 us)
where the time goes:
time: 900 us; the launch traced here: 891 us
  matrix products  346 us (38%)
  local copies, waits for them, and re-layouts  278 us (31%)
  other arithmetic  141 us (16%)
  waiting for transfers between devices  80.9 us (9%)
  starting transfers between devices  42.7 us (5%)
    dot_general x27, matrix products, conv_local(): jnp.einsum('oc,fchw->fohw', kernel[row_tap, col_tap], window, preferred_e...  345 us
    concatenate x7, other arithmetic, padded_2(): block = jnp.concatenate([low, block, high], axis=dim)  116 us
    slice x9, local copies, waits for them, and re-layouts, padded_2(): lax.slice_in_dim(block, block.shape[dim] - width, None, axis=dim)  71.8 us
    slice x5, local copies, waits for them, and re-layouts, padded_2(): lax.slice_in_dim(block, 0, width, axis=dim)  69.3 us
    ppermute x8, waiting for transfers between devices, padded_2(): lax.ppermute(lax.slice_in_dim(block, block.shape[dim] - width, None, axis...  56.7 us
    ppermute x4, local copies, waits for them, and re-layouts, padded_2(): lax.ppermute(lax.slice_in_dim(block, block.shape[dim] - width, None, axis...  55.5 us
    ppermute x4, local copies, waits for them, and re-layouts, padded_2(): lax.ppermute(lax.slice_in_dim(block, 0, width, axis=dim), axis, backward)  55.5 us
    ppermute x8, starting transfers between devices, padded_2(): lax.ppermute(lax.slice_in_dim(block, block.shape[dim] - width, None, axis...  21.8 us
  transfers between devices with their start and end apart: 18, of which 9 were waited for; matrix products, arithmetic and copies ran while one was open for 70% of the time, Pallas kernels for 0%

commit v1 on v0

v1 whole, which is shorter than its diff:
```python
import functools

import jax
import jax.numpy as jnp
import numpy as np
from jax import lax
from jax.experimental import pallas as pl
from jax.experimental.pallas import tpu as pltpu
from jax.sharding import PartitionSpec as P

TAPS = 31
KBINS = 8
BF = jnp.bfloat16
F32 = jnp.float32
LANES = 128
GROUP = 16
PITCH = 32


def padded_2(block, sides, width):
    for axis, dim in sides:
        count = lax.axis_size(axis)
        forward = [(i, i + 1) for i in range(count - 1)]
        backward = [(target, source) for source, target in forward]
        low = lax.ppermute(
            lax.slice_in_dim(block, block.shape[dim] - width, None, axis=dim), axis, forward
        )
        high = lax.ppermute(lax.slice_in_dim(block, 0, width, axis=dim), axis, backward)
        block = jnp.concatenate([low, block, high], axis=dim)
    return block


def conv_local(padded, kernel):
    height = padded.shape[2] - 2
    width = padded.shape[3] - 2
    total = None
    for row_tap in range(3):
        for col_tap in range(3):
            window = padded[:, :, row_tap : row_tap + height, col_tap : col_tap + width]
            term = jnp.einsum(
                "oc,fchw->fohw",
                kernel[row_tap, col_tap],
                window,
                preferred_element_type=jnp.float32,
            )
            total = term if total is None else total + term
    return total


def with_rim(values):
    return padded_2(values, (("skyx", 2), ("skyy", 3)), 1)


def plain_score(xb, w_first, w_second, w_third, w_last):
    hidden = xb[:, None]
    for kernel in (w_first, w_second, w_third):
        hidden = jax.nn.silu(conv_local(with_rim(hidden), kernel)).astype(jnp.bfloat16)
    return conv_local(with_rim(hidden), w_last)[:, 0]


def silu_half(u):
    return (u + u * jnp.tanh(u)).astype(BF)


def net_body(tiles_x, tiles_y, rows_loc, chans, cols_loc, chunk,
             x_ref, base_ref, w2_ref, w3_ref, wl_ref, out_ref,
             x1_ref, w1_ref, w2s_ref, w3s_ref, h1_ref, h2_ref, nb_ref, h3_ref, ot_ref):
    rows = tiles_x * rows_loc
    cols = tiles_y * cols_loc
    pairs = cols // 2
    groups = cols // GROUP
    per_block = cols_loc // GROUP
    feat = w2_ref.shape[-1]
    two = 2 * feat
    lane = lax.broadcasted_iota(jnp.int32, (chans, LANES), 1)

    k_row = lax.broadcasted_iota(jnp.int32, (4 * PITCH, 16), 0)
    k_col = lax.broadcasted_iota(jnp.int32, (4 * PITCH, 16), 1)
    base = base_ref[...]
    for p in range(GROUP // 2):
        pick = (k_row // PITCH == k_col // 4) & (k_row % PITCH == k_col % 4 + 2 * p)
        w1_ref[p] = jnp.dot(pick.astype(BF), base, preferred_element_type=F32).astype(BF)

    zero = jnp.zeros((feat, feat), BF)
    for src, dst in ((w2_ref, w2s_ref), (w3_ref, w3s_ref)):
        for w in range(4):
            for blk in range(4):
                for a in range(2):
                    ta = w - a
                    parts = []
                    for b in range(2):
                        tb = (1 - b, 2 - b, 3 - b, -b)[blk]
                        ok = 0 <= ta < 3 and 0 <= tb < 3
                        parts.append(src[ta * 3 + tb] if ok else zero)
                    k0 = (w * 4 + blk) * feat
                    dst[k0 : k0 + feat, a * two : (a + 1) * two] = jnp.concatenate(parts, axis=1)

    rim = jnp.zeros((rows, 1, chans, two), BF)
    for ref in (h1_ref, h2_ref):
        ref[:, 0:1] = rim
        ref[:, pairs + 1 : pairs + 2] = rim
    edge = jnp.zeros((ot_ref.shape[0], LANES), F32)
    ot_ref[:, 0:LANES] = edge
    ot_ref[:, LANES + pairs * chans :] = edge

    def window_block(cb, _):
        lo = jnp.maximum(cb - 1, 0)
        hi = jnp.minimum(cb + 1, tiles_y - 1)
        has_lo = (cb > 0).astype(F32)
        has_hi = (cb < tiles_y - 1).astype(F32)
        for gl in range(per_block):
            acc = [jnp.zeros((chans, LANES), F32) for _ in range(rows // 2)]
            for r in range(rows):
                src = (r // rows_loc) * tiles_y
                rl = r % rows_loc
                cur = x_ref[(src + cb) * rows_loc + rl].astype(F32)
                for w in range(4):
                    rb = r + 1 - w
                    if rb % 2 or not 0 <= rb < rows:
                        continue
                    shift = (PITCH * w - (GROUP * gl - 1)) % LANES
                    val = pltpu.roll(cur, shift, 1)
                    if gl == 0:
                        prev = x_ref[(src + lo) * rows_loc + rl].astype(F32) * has_lo
                        val = jnp.where(lane == PITCH * w, pltpu.roll(prev, shift, 1), val)
                    if gl == per_block - 1:
                        nxt = x_ref[(src + hi) * rows_loc + rl].astype(F32) * has_hi
                        val = jnp.where(
                            lane == PITCH * w + GROUP + 1, pltpu.roll(nxt, shift, 1), val
                        )
                    keep = (lane >= PITCH * w) & (lane < PITCH * w + GROUP + 2)
                    acc[rb // 2] = jnp.where(keep, val, acc[rb // 2])
            for half in range(rows // 2):
                x1_ref[half, cb * per_block + gl] = acc[half].astype(BF)
        return 0

    lax.fori_loop(0, tiles_y, window_block, 0)

    def first(step, _):
        half = step // (GROUP // 2)
        p = step % (GROUP // 2)
        lhs = x1_ref[half].reshape(groups * chans, 4 * PITCH)
        u = jnp.dot(lhs, w1_ref[p], preferred_element_type=F32)
        h = silu_half(u).reshape(groups, chans, 2 * two)
        for g in range(groups):
            for a in range(2):
                h1_ref[2 * half + a, 1 + g * (GROUP // 2) + p] = h[g, :, a * two : (a + 1) * two]
        return 0

    lax.fori_loop(0, (rows // 2) * (GROUP // 2), first, 0)

    lane_nb = lax.broadcasted_iota(jnp.int32, (chunk, chans, two), 2)

    def layer(src, weights, start, emit):
        for r in range(rows):
            nb_ref[r] = jnp.where(
                lane_nb < feat, src[r, pl.ds(start + 2, chunk)], src[r, pl.ds(start, chunk)]
            )
        for rb in range(0, rows, 2):
            first_w = 1 if rb == 0 else 0
            last_w = 3 if rb + 2 >= rows else 4
            parts = []
            for w in range(first_w, last_w):
                r = rb - 1 + w
                parts.append(src[r, pl.ds(start + 1, chunk)].reshape(chunk * chans, two))
                parts.append(nb_ref[r].reshape(chunk * chans, two))
            lhs = jnp.concatenate(parts, axis=1)
            u = jnp.dot(
                lhs, weights[first_w * 2 * two : last_w * 2 * two], preferred_element_type=F32
            )
            h = silu_half(u)
            for a in range(2):
                emit(rb + a, h[:, a * two : (a + 1) * two].reshape(chunk, chans, two))

    def second(step, _):
        start = step * chunk

        def emit(r, h):
            h2_ref[r, pl.ds(start + 1, chunk)] = h

        layer(h1_ref, w2s_ref, start, emit)
        return 0

    lax.fori_loop(0, pairs // chunk, second, 0)

    def third(step, _):
        start = step * chunk

        def emit(r, h):
            h3_ref[r] = h

        layer(h2_ref, w3s_ref, start, emit)
        full = jnp.concatenate(
            [h3_ref[r].reshape(chunk * chans, two) for r in range(rows)], axis=1
        )
        out = lax.dot_general(
            wl_ref[...], full, (((1,), (1,)), ((), ())), preferred_element_type=F32
        )
        width = chunk * chans
        ot_ref[:, pl.ds(pl.multiple_of(LANES + step * width, LANES), width)] = out
        return 0

    lax.fori_loop(0, pairs // chunk, third, 0)

    own_rows = 2 * rows
    per_tile = 2 * rows_loc
    width = (cols_loc // 2) * chans
    sub = lax.broadcasted_iota(jnp.int32, (own_rows, width), 0) % per_tile
    for ty in range(tiles_y):
        at = LANES + ty * width
        own = ot_ref[:own_rows, at : at + width]
        before = ot_ref[own_rows:, at - chans : at - chans + width]
        after = ot_ref[own_rows:, at + chans : at + chans + width]
        total = own + jnp.where(sub < rows_loc, before, after)
        for tx in range(tiles_x):
            out_ref[tx * tiles_y + ty] = total[tx * per_tile : (tx + 1) * per_tile].astype(BF)


def net_constants(w_first, w_second, w_third, w_last, rows, rows_loc):
    feat = w_second.shape[-1]
    half = jnp.asarray(0.5, BF)
    first = (w_first[..., 0] * half).astype(BF)
    base = jnp.stack(
        [
            jnp.pad(first, ((a, 1 - a), (b, 1 - b), (0, 0)))
            for a in range(2)
            for b in range(2)
        ],
        axis=2,
    ).reshape(16, 4 * feat)
    second = jnp.swapaxes(w_second * half, 2, 3).reshape(9, feat, feat)
    third = jnp.swapaxes(w_third * half, 2, 3).reshape(9, feat, feat)
    pick = np.zeros((2, rows // rows_loc, 2, rows_loc, rows, 2, 9), np.float32)
    for r_out in range(rows):
        for r_in in range(max(r_out - 1, 0), min(r_out + 2, rows)):
            ta = r_in - r_out + 1
            for b_in in range(2):
                for b in range(2):
                    tile, rl = divmod(r_out, rows_loc)
                    pick[0, tile, b, rl, r_in, b_in, ta * 3 + b_in - b + 1] = 1
                    tb = b_in - 1 if b == 0 else b_in + 2
                    if 0 <= tb < 3:
                        pick[1, tile, b, rl, r_in, b_in, ta * 3 + tb] = 1
    last = jnp.dot(
        jnp.asarray(pick.reshape(-1, 9), BF),
        w_last.reshape(9, feat),
        preferred_element_type=F32,
    ).astype(BF).reshape(4 * rows, rows * 2 * feat)
    return base, second, third, last


def net_score(spread, consts, tiles_x, tiles_y, rows_loc, interpret=False):
    base, second, third, last = consts
    chans, cols_loc = spread.shape[1:]
    feat = second.shape[-1]
    rows = tiles_x * rows_loc
    cols = tiles_y * cols_loc
    pairs = cols // 2
    chunk = next(c for c in (32, 16, 8) if pairs % c == 0)
    groups = cols // GROUP
    vmem = pltpu.MemorySpace.VMEM
    spec = pl.BlockSpec(memory_space=vmem)
    return pl.pallas_call(
        functools.partial(net_body, tiles_x, tiles_y, rows_loc, chans, cols_loc, chunk),
        out_shape=jax.ShapeDtypeStruct(
            (tiles_x * tiles_y, 2 * rows_loc, cols_loc // 2 * chans), BF
        ),
        in_specs=[spec] * 5,
        out_specs=spec,
        scratch_shapes=[
            pltpu.VMEM((rows // 2, groups, chans, 4 * PITCH), BF),
            pltpu.VMEM((GROUP // 2, 4 * PITCH, 4 * feat), BF),
            pltpu.VMEM((16 * feat, 4 * feat), BF),
            pltpu.VMEM((16 * feat, 4 * feat), BF),
            pltpu.VMEM((rows, pairs + 2, chans, 2 * feat), BF),
            pltpu.VMEM((rows, pairs + 2, chans, 2 * feat), BF),
            pltpu.VMEM((rows, chunk, chans, 2 * feat), BF),
            pltpu.VMEM((rows, chunk, chans, 2 * feat), BF),
            pltpu.VMEM((4 * rows, 2 * LANES + pairs * chans), F32),
        ],
        compiler_params=pltpu.CompilerParams(vmem_limit_bytes=58 << 20),
        name="net",
        interpret=interpret,
    )(spread, base, second, third, last)


PAD = 16


def spec_body(chans, block, x_ref, beam_ref, obs_ref, var_ref, kbin_ref, taps_ref, out_ref,
              xp_ref, rp_ref, wp_ref, bp_ref, bb_ref, tap_ref):
    half = TAPS // 2
    cols = x_ref.shape[-1]
    edge = jnp.zeros((PAD, cols), F32)
    for ref in (xp_ref, rp_ref, wp_ref, bp_ref):
        ref[0:PAD] = edge
        ref[PAD + chans :] = edge
    for tap in range(TAPS):
        bb_ref[tap, 0:PAD] = edge
        bb_ref[tap, PAD + chans :] = edge
    xp_ref[PAD : PAD + chans] = x_ref[...].astype(F32)
    bins = kbin_ref[...]
    for tap in range(TAPS):
        val = jnp.zeros((1, cols), F32)
        for k in range(KBINS):
            val = jnp.where(bins == k, taps_ref[k, tap], val)
        tap_ref[tap : tap + 1] = val
    steps = chans // block

    def span(start):
        return pl.ds(start, block)

    def model(i, _):
        f0 = pl.multiple_of(i * block, block)
        acc = jnp.zeros((block, cols), F32)
        beam = beam_ref[span(f0)]
        for tap in range(TAPS):
            wide = jnp.broadcast_to(beam[:, tap : tap + 1], (block, cols))
            bb_ref[tap, span(PAD + f0)] = wide
            acc = acc + wide * xp_ref[span(f0 + PAD - half + tap)]
        rp_ref[span(PAD + f0)] = acc - obs_ref[span(f0)]
        return 0

    lax.fori_loop(0, steps, model, 0)

    def wedge(i, _):
        f0 = pl.multiple_of(i * block, block)
        acc = jnp.zeros((block, cols), F32)
        for tap in range(TAPS):
            acc = acc + tap_ref[tap : tap + 1] * rp_ref[span(f0 + PAD - half + tap)]
        wp_ref[span(PAD + f0)] = acc * var_ref[span(f0)]
        return 0

    lax.fori_loop(0, steps, wedge, 0)

    def back(i, _):
        f0 = pl.multiple_of(i * block, block)
        acc = jnp.zeros((block, cols), F32)
        for tap in range(TAPS):
            acc = acc + tap_ref[tap : tap + 1] * wp_ref[span(f0 + PAD + half - tap)]
        bp_ref[span(PAD + f0)] = acc
        return 0

    lax.fori_loop(0, steps, back, 0)

    def grad(i, _):
        f0 = pl.multiple_of(i * block, block)
        acc = jnp.zeros((block, cols), F32)
        for tap in range(TAPS):
            at = span(f0 + PAD + half - tap)
            acc = acc + bb_ref[tap, at] * bp_ref[at]
        out_ref[span(f0)] = acc.astype(BF)
        return 0

    lax.fori_loop(0, steps, grad, 0)


def spec_grad(spectra, beam, observed, inv_variance, kbin, wedge_taps, interpret=False):
    chans, cols = spectra.shape
    spec = pl.BlockSpec(memory_space=pltpu.MemorySpace.VMEM)
    smem = pl.BlockSpec(memory_space=pltpu.MemorySpace.SMEM)
    tall = pltpu.VMEM((chans + 2 * PAD, cols), F32)
    return pl.pallas_call(
        functools.partial(spec_body, chans, 64 if chans % 64 == 0 else 8),
        out_shape=jax.ShapeDtypeStruct((chans, cols), BF),
        in_specs=[spec] * 5 + [smem],
        out_specs=spec,
        scratch_shapes=[
            tall, tall, tall, tall,
            pltpu.VMEM((TAPS, chans + 2 * PAD, cols), F32),
            pltpu.VMEM((TAPS + 1, cols), F32),
        ],
        compiler_params=pltpu.CompilerParams(vmem_limit_bytes=32 << 20),
        name="spectral",
        interpret=interpret,
    )(spectra, beam, observed, inv_variance, kbin, wedge_taps)


def start_body(rows_loc, field_ref, out_ref):
    chans = out_ref.shape[1]
    for r in range(rows_loc):
        out_ref[r] = field_ref[pl.ds(r, chans, stride=rows_loc)].astype(BF)


def row_major(field, interpret=False):
    chans, rows_loc, cols = field.shape
    spec = pl.BlockSpec(memory_space=pltpu.MemorySpace.VMEM)
    return pl.pallas_call(
        functools.partial(start_body, rows_loc),
        out_shape=jax.ShapeDtypeStruct((rows_loc, chans, cols), BF),
        in_specs=[spec],
        out_specs=spec,
        name="rows",
        interpret=interpret,
    )(field.reshape(chans * rows_loc, cols))


def last_body(rows_loc, field_ref, noise_ref, step_ref, grad_ref, score_ref, out_ref, lhs_ref):
    sources, _, wide = score_ref.shape
    chans, cols = grad_ref.shape[1:]
    sub = chans // sources
    mine = lax.broadcasted_iota(jnp.int32, (sub, wide), 1) % sub == lax.broadcasted_iota(
        jnp.int32, (sub, wide), 0
    )
    k = lax.broadcasted_iota(jnp.int32, (2 * wide, cols), 0)
    c = lax.broadcasted_iota(jnp.int32, (2 * wide, cols), 1)
    place = (2 * ((k % wide) // sub) + k // wide == c).astype(F32).astype(BF)
    zero = jnp.zeros((sub, wide), F32)
    for s in range(sources):
        block = score_ref[s].astype(F32)
        for r in range(rows_loc):
            for b in range(2):
                row = block[b * rows_loc + r : b * rows_loc + r + 1]
                lhs_ref[r, s * sub : (s + 1) * sub, b * wide : (b + 1) * wide] = jnp.where(
                    mine, jnp.broadcast_to(row, (sub, wide)), zero
                ).astype(BF)
    step = jnp.broadcast_to(step_ref[...], (chans, cols))
    spread = jnp.sqrt(2.0 * step)
    for r in range(rows_loc):
        score = jnp.dot(lhs_ref[r], place, preferred_element_type=F32)
        at = pl.ds(r, chans, stride=rows_loc)
        out_ref[at] = (
            field_ref[at]
            + step * (score - grad_ref[r].astype(F32))
            + spread * noise_ref[at]
        )


def finish(field, noise, step_size, grad, score, interpret=False):
    chans, rows_loc, cols = field.shape
    spec = pl.BlockSpec(memory_space=pltpu.MemorySpace.VMEM)
    wide = score.shape[-1]
    out = pl.pallas_call(
        functools.partial(last_body, rows_loc),
        out_shape=jax.ShapeDtypeStruct((chans * rows_loc, cols), F32),
        in_specs=[spec] * 5,
        out_specs=spec,
        scratch_shapes=[pltpu.VMEM((rows_loc, chans, 2 * wide), BF)],
        name="finish",
        interpret=interpret,
    )(
        field.reshape(chans * rows_loc, cols),
        noise.reshape(chans * rows_loc, cols),
        step_size[:, None],
        grad,
        score,
    )
    return out.reshape(chans, rows_loc, cols)


def per_device(
    field,
    noise,
    step_size,
    w_first,
    w_second,
    w_third,
    w_last,
    observed,
    inv_variance,
    offsets,
    beam_table,
    kbin,
    wedge_taps,
):
    chans_loc, rows_loc, cols_loc = field.shape
    tiles_x, tiles_y = lax.axis_size("skyx"), lax.axis_size("skyy")
    tiles = tiles_x * tiles_y
    freq = lax.axis_size("freq")
    chans = observed.shape[0]
    rows_spec = observed.shape[1]
    fast = (
        chans_loc % (16 * tiles) == 0
        and rows_loc % 2 == 0
        and cols_loc % LANES == 0
        and 2 * w_second.shape[-1] == LANES
        and chans_loc // tiles * tiles_x * rows_loc * tiles_y * cols_loc <= 1 << 16
    )

    rows_first = row_major(field)
    if fast:
        spread = lax.all_to_all(
            rows_first.reshape(rows_loc, chans_loc, cols_loc),
            ("skyx", "skyy"), split_axis=1, concat_axis=0, tiled=True,
        )
    spectra = lax.all_to_all(rows_first, "freq", split_axis=0, concat_axis=0, tiled=True)
    spectra = spectra.reshape(freq, rows_spec, chans_loc, cols_loc)

    grads = []
    for r in range(rows_spec):
        beam = lax.dynamic_slice(beam_table, (offsets[r], 0), (chans, TAPS))
        grads.append(
            spec_grad(
                spectra[:, r].reshape(chans, cols_loc),
                beam,
                observed[:, r],
                inv_variance[:, r],
                kbin[r : r + 1],
                wedge_taps,
            ).reshape(freq, chans_loc, cols_loc)
        )
    grad = jnp.stack(grads, axis=1).reshape(freq * rows_spec, chans_loc, cols_loc)
    grad = lax.all_to_all(grad, "freq", split_axis=0, concat_axis=0, tiled=True)

    if fast:
        consts = net_constants(
            w_first, w_second, w_third, w_last, tiles_x * rows_loc, rows_loc
        )
        score = net_score(spread, consts, tiles_x, tiles_y, rows_loc)
        score = lax.all_to_all(score, ("skyx", "skyy"), split_axis=0, concat_axis=0, tiled=True)
        return finish(field, noise, step_size, grad, score)
    score = plain_score(field.astype(BF), w_first, w_second, w_third, w_last)
    steps = step_size[:, None, None]
    grad = jnp.swapaxes(grad, 0, 1).astype(F32)
    return field + steps * (score - grad) + jnp.sqrt(2.0 * steps) * noise


def solution(mesh):
    return jax.shard_map(
        per_device,
        mesh=mesh,
        in_specs=(
            P("freq", "skyx", "skyy"),
            P("freq", "skyx", "skyy"),
            P("freq"),
            P(),
            P(),
            P(),
            P(),
            P(None, ("skyx", "freq"), "skyy"),
            P(None, ("skyx", "freq"), "skyy"),
            P(("skyx", "freq")),
            P(),
            P(("skyx", "freq"), "skyy"),
            P(),
        ),
        out_specs=P("freq", "skyx", "skyy"),
        check_vma=False,
    )
```

time: 900 us -> 79.5 us (0.09)
  matrix products: 346 us -> 0.2 us
  local copies, waits for them, and re-layouts: 278 us -> 9.99 us
  other arithmetic: 141 us -> 0.06 us
  waiting for transfers between devices: 80.9 us -> 7.24 us
  Pallas kernels: 0 us -> 41.5 us
  starting transfers between devices: 42.7 us -> 19.1 us
    dot_general x28 -> x1, matrix products: 346 us -> 0.2 us  [net_constants(): jnp.dot(jnp.asarray(pick.reshape(-1, 9), BF), w_last.reshape(9, feat), pr...]
    slice x49 -> x0, local copies, waits for them, and re-layouts: 154 us -> none  [the longest x9 71.8 us: padded_2(): lax.slice_in_dim(block, block.shape[dim] - width, None, axis=dim)]
    concatenate x7 -> x0, other arithmetic: 116 us -> none  [padded_2(): block = jnp.concatenate([low, block, high], axis=dim)]
    ppermute x8 -> x0, local copies, waits for them, and re-layouts: 111 us -> none  [the longest x4 55.5 us: padded_2(): lax.ppermute(lax.slice_in_dim(block, block.shape[dim] - width, None, axis...]
    ppermute x16 -> x0, waiting for transfers between devices: 75 us -> none  [the longest x8 56.7 us: padded_2(): lax.ppermute(lax.slice_in_dim(block, block.shape[dim] - width, None, axis...]
    pallas_call x0 -> x4, Pallas kernels: none -> 41.5 us  [the longest x1 30.3 us: net_score(): pl.pallas_call(functools.partial(net_body, tiles_x, tiles_y, rows_loc, ch...]
    ppermute x16 -> x0, starting transfers between devices: 32.4 us -> none  [the longest x8 21.8 us: padded_2(): lax.ppermute(lax.slice_in_dim(block, block.shape[dim] - width, None, axis...]
    convert_element_type x4 -> x0, other arithmetic: 17 us -> none  [the longest x1 12.8 us: per_device(): jax.nn.silu(conv_local(with_rim(hidden), kernel)).astype(jnp.bfloat16)]
  transfers between devices with their start and end apart: 18 -> 4, of which waited for: 9 -> 2; matrix products, arithmetic and copies ran while one was open for 70% -> 6% of each run, Pallas kernels for 0% -> 47%
where the time goes in v1:
time: 79.5 us; the launch traced here: 78.9 us
  Pallas kernels  41.5 us (52%)
  starting transfers between devices  19.1 us (24%)
  local copies, waits for them, and re-layouts  9.99 us (13%)
  waiting for transfers between devices  7.24 us (9%)
  between operations  0.85 us (1%)
    pallas_call x1, Pallas kernels, net_score(): pl.pallas_call(functools.partial(net_body, tiles_x, tiles_y, rows_loc, ch...  30.3 us
    pallas_call x1, Pallas kernels, spec_grad(): pl.pallas_call(functools.partial(spec_body, chans, 64 if chans % 64 == 0...  6.78 us
    all_to_all x1, starting transfers between devices, per_device(): grad = lax.all_to_all(grad, 'freq', split_axis=0, concat_axis=0, tiled=True)  5.36 us
    all_to_all x1, starting transfers between devices, per_device(): lax.all_to_all(rows_first.reshape(rows_loc, chans_loc, cols_loc), ('skyx'...  5.33 us
    all_to_all x1, waiting for transfers between devices, per_device(): grad = lax.all_to_all(grad, 'freq', split_axis=0, concat_axis=0, tiled=True)  5.04 us
    all_to_all x1, starting transfers between devices, per_device(): lax.all_to_all(rows_first, 'freq', split_axis=0, concat_axis=0, tiled=True)  4.87 us
    unnamed x27, local copies, waits for them, and re-layouts  3.66 us
    all_to_all x1, starting transfers between devices, per_device(): lax.all_to_all(score, ('skyx', 'skyy'), split_axis=0, concat_axis=0, tile...  3.5 us
  transfers between devices with their start and end apart: 4, of which 2 were waited for; matrix products, arithmetic and copies ran while one was open for 6% of the time, Pallas kernels for 47%

profile of v1, /device:TPU:0, one launch (start us, length us, event | category | flops | bytes accessed | tf_op | source)
XLA Modules:
  0.0 78.9 jit_solution(13333325772524426647)
XLA Ops:
  0.0 0.0 copy-start
  0.0 1.7 %rows.1 = bf16[4,128,128]{2,1,0:T(8,128)(2,1)} custom-call(f32[512,128]{1,0:T(8,128)} %bitcast.39), custom_call_target="tpu_custom_call" | custom-call | tf_op jit(solution)/shard_map/rows/pallas_call | solution.py:388
  1.7 1.7 %copy.30 = bf16[4,128,128]{2,0,1:T(4,128)(2,1)} copy(bf16[4,128,128]{2,1,0:T(8,128)(2,1)} %rows.1) | data formatting | bytes 262144 | tf_op jit(solution)/shard_map/rows/pallas_call | solution.py:388
  3.3 0.0 copy-start.11
  3.3 0.0 copy-start.7
  3.3 5.3 %all-to-all-start.2 = ((bf16[4,128,128]{2,0,1:T(4,128)(2,1)}), bf16[4,128,128]{2,0,1:T(4,128)(2,1)S(1)}, u32[]{:S(2)}, u32[]{:S(2)}) async-start(bf16[4,128,128]{2,0,1:T(4,128)(2,1)} %copy.30), calls=%async_computation.2 | async-start | bytes 262144 | tf_op jit(solution)/shard_map/all_to_all | solution.py:482
  8.6 0.0 copy-done.11
  8.7 0.0 copy-done.7
  8.7 0.0 copy-start.8
  8.7 0.9 %copy-done.8 = bf16[3,3,64,64]{3,2,1,0:T(8,128)(2,1)S(1)} copy-done((bf16[3,3,64,64]{3,2,1,0:T(8,128)(2,1)S(1)}, bf16[3,3,64,64]{3,2,1,0:T(8,128)(2,1)}, u32[]{:S(2)}) %copy-start.8) | copy-done | bytes 73752
  9.7 0.7 reshape.29.base_ref
  10.3 0.8 %copy.33 = bf16[3,3,64,64]{3,2,1,0:T(8,128)(2,1)} copy(bf16[3,3,64,64]{2,3,1,0:T(8,128)(2,1)S(1)} %multiply_bitcast_fusion.1) | data formatting | bytes 147456 | tf_op jit(solution)/shard_map/transpose | solution.py:231
  11.1 0.0 copy-start.10
  11.1 0.8 copy.34
  11.9 0.0 copy-done.10
  12.0 0.0 copy-start.9
  12.0 2.2 %all-to-all-done.2 = bf16[4,128,128]{2,0,1:T(4,128)(2,1)S(1)} async-done(((bf16[4,128,128]{2,0,1:T(4,128)(2,1)}), bf16[4,128,128]{2,0,1:T(4,128)(2,1)S(1)}, u32[]{:S(2)}, u32[]{:S(2)}) %all-to-all-start.2) | async-done | bytes 131104 | tf_op jit(solution)/shard_map/all_to_all | solution.py:482
  14.1 4.9 %all-to-all-start = ((bf16[4,128,128]{2,1,0:T(8,128)(2,1)}), bf16[4,128,128]{2,1,0:T(8,128)(2,1)S(1)}, u32[]{:S(2)}, u32[]{:S(2)}) async-start(bf16[4,128,128]{2,1,0:T(8,128)(2,1)} %rows.1), calls=%async_computation | async-start | bytes 262144 | tf_op jit(solution)/shard_map/all_to_all | solution.py:486
  19.0 0.0 copy-done.9
  19.0 0.2 convolution_convert_fusion
  19.2 0.1 copy.35
  19.4 0.8 reshape.33.wl_ref
  20.1 0.7 copy.31
  20.8 30.3 %net.1 = bf16[8,8,1024]{2,1,0:T(8,128)(2,1)} custom-call(bf16[32,16,128]{2,1,0:T(8,128)(2,1)} %bitcast.43, bf16[16,256]{1,0:T(8,128)(2,1)} %reshape.29.base_ref, bf16[9,64,64]{2,1,0:T(8,128)(2,1)} %bitcast.41, bf16[9,64,64]{2,1,0:T(8,128)(2,1)} %bitcast.42, bf16[32,1024]{1,0:T(8,128)(2,1)} %reshape.33.wl_ref), custom_call_target="tpu_custom_call" | custom-call | tf_op jit(solution)/shard_map/net/pallas_call | solution.py:263
  51.1 0.0 all-to-all-done
  51.1 0.0 copy-start.2
  51.1 3.5 %all-to-all-start.3 = ((bf16[8,8,1024]{2,1,0:T(8,128)(2,1)}), bf16[8,8,1024]{2,1,0:T(8,128)(2,1)S(1)}, u32[]{:S(2)}, u32[]{:S(2)}) async-start(bf16[8,8,1024]{2,1,0:T(8,128)(2,1)} %net.1), calls=%async_computation.3 | async-start | bytes 262144 | tf_op jit(solution)/shard_map/all_to_all | solution.py:510
  54.6 0.0 copy-start.1
  55.3 0.0 copy-done
  55.3 0.1 constant_dynamic-slice_fusion
  55.4 0.1 copy.37.beam_ref
  55.5 0.0 copy-start.3
  55.5 0.0 copy-start.4
  55.6 0.0 copy-done.2
  55.6 0.0 copy-done.1
  55.6 0.7 copy-done.3
  56.2 0.0 copy-done.4
  56.2 6.8 %spectral.1 = bf16[512,128]{1,0:T(8,128)(2,1)} custom-call(bf16[512,128]{1,0:T(8,128)(2,1)S(1)} %bitcast.36, f32[512,31]{1,0:T(8,128)S(1)} %copy.37.beam_ref, f32[512,128]{1,0:T(8,128)S(1)} %bitcast.37, f32[512,128]{1,0:T(8,128)S(1)} %bitcast.38, s32[1,128]{1,0:T(1,128)S(1)} %copy-done.4, f32[8,31]{1,0:T(8,128)S(1)} %copy-done.3), custom_call_target="tpu_custom_call" | custom-call | tf_op jit(solution)/shard_map/spectral/pallas_call | solution.py:363
  63.0 0.0 all-to-all-done.3.score_ref
  63.0 0.0 copy-start.5
  63.0 0.6 copy-done.5
  63.7 5.4 %all-to-all-start.1 = ((bf16[4,128,128]{2,1,0:T(8,128)(2,1)}), bf16[4,128,128]{2,1,0:T(8,128)(2,1)S(1)}, u32[]{:S(2)}, u32[]{:S(2)}) async-start(bf16[4,128,128]{2,1,0:T(8,128)(2,1)} %bitcast.7), calls=%async_computation.1 | async-start | bytes 262144 | tf_op jit(solution)/shard_map/all_to_all | solution.py:503
  69.0 0.0 copy-start.12
  69.0 0.7 copy-done.12
  69.7 0.7 copy.36.step_ref
  70.4 5.0 %all-to-all-done.1.grad_ref = bf16[4,128,128]{2,1,0:T(8,128)(2,1)S(1)} async-done(((bf16[4,128,128]{2,1,0:T(8,128)(2,1)}), bf16[4,128,128]{2,1,0:T(8,128)(2,1)S(1)}, u32[]{:S(2)}, u32[]{:S(2)}) %all-to-all-start.1) | async-done | bytes 131104 | tf_op jit(solution)/shard_map/all_to_all | solution.py:503
  75.5 0.0 copy-start.6
  75.5 0.6 copy-done.6
  76.1 2.8 %finish.1 = f32[512,128]{1,0:T(8,128)} custom-call(f32[512,128]{1,0:T(8,128)} %bitcast.40, f32[512,128]{1,0:T(8,128)} %bitcast.45, f32[128,1]{1,0:T(8,128)} %copy.36.step_ref, bf16[4,128,128]{2,1,0:T(8,128)(2,1)} %copy-done.6, bf16[8,8,1024]{2,1,0:T(8,128)(2,1)} %copy-done.5), custom_call_target="tpu_custom_call" | custom-call | tf_op jit(solution)/shard_map/finish/pallas_call | solution.py:433
  (7 shorter events, 0.1 us)
Async XLA Ops:
  0.0 55.3 %copy-start = (f32[1024,31]{0,1:T(8,128)S(1)}, f32[1024,31]{0,1:T(8,128)}, u32[]{:S(2)}) copy-start(f32[1024,31]{0,1:T(8,128)} %param.24) | copy-start | bytes 380932
  3.3 5.3 %copy-start.11 = (bf16[3,3,64,1]{2,1,3,0:T(4,128)(2,1)S(1)}, bf16[3,3,64,1]{2,1,3,0:T(4,128)(2,1)}, u32[]{:S(2)}) copy-start(bf16[3,3,64,1]{2,1,3,0:T(4,128)(2,1)} %param.17) | copy-start | bytes 3460
  3.3 5.4 %copy-start.7 = (bf16[3,3,64,64]{3,2,1,0:T(8,128)(2,1)S(1)}, bf16[3,3,64,64]{3,2,1,0:T(8,128)(2,1)}, u32[]{:S(2)}) copy-start(bf16[3,3,64,64]{3,2,1,0:T(8,128)(2,1)} %param.18) | copy-start | bytes 221188
  3.3 10.8 %all-to-all-start.2 = ((bf16[4,128,128]{2,0,1:T(4,128)(2,1)}), bf16[4,128,128]{2,0,1:T(4,128)(2,1)S(1)}, u32[]{:S(2)}, u32[]{:S(2)}) async-start(bf16[4,128,128]{2,0,1:T(4,128)(2,1)} %copy.30), calls=%async_computation.2 | async-start | bytes 262144 | tf_op jit(solution)/shard_map/all_to_all | solution.py:482
  8.7 0.9 %copy-start.8 = (bf16[3,3,64,64]{3,2,1,0:T(8,128)(2,1)S(1)}, bf16[3,3,64,64]{3,2,1,0:T(8,128)(2,1)}, u32[]{:S(2)}) copy-start(bf16[3,3,64,64]{3,2,1,0:T(8,128)(2,1)} %param.19) | copy-start | bytes 221188
  11.1 0.8 %copy-start.10 = (bf16[3,3,1,64]{3,1,2,0:T(4,128)(2,1)S(1)}, bf16[3,3,1,64]{3,1,2,0:T(4,128)(2,1)}, u32[]{:S(2)}) copy-start(bf16[3,3,1,64]{3,1,2,0:T(4,128)(2,1)} %param.20) | copy-start | bytes 3460
  12.0 7.1 %copy-start.9 = (bf16[512,9]{1,0:T(8,128)(2,1)S(1)}, bf16[512,9]{1,0:T(8,128)(2,1)}, u32[]{:S(2)}) copy-start(bf16[512,9]{1,0:T(8,128)(2,1)} %constant.11.clone) | copy-start | bytes 27652
  14.1 36.9 %all-to-all-start = ((bf16[4,128,128]{2,1,0:T(8,128)(2,1)}), bf16[4,128,128]{2,1,0:T(8,128)(2,1)S(1)}, u32[]{:S(2)}, u32[]{:S(2)}) async-start(bf16[4,128,128]{2,1,0:T(8,128)(2,1)} %rows.1), calls=%async_computation | async-start | bytes 262144 | tf_op jit(solution)/shard_map/all_to_all | solution.py:486
  51.1 4.5 %copy-start.2 = (f32[512,1,128]{2,1,0:T(1,128)S(1)}, f32[512,1,128]{2,1,0:T(1,128)}, u32[]{:S(2)}) copy-start(f32[512,1,128]{2,1,0:T(1,128)} %param.22) | copy-start | bytes 786436
  51.1 11.9 %all-to-all-start.3 = ((bf16[8,8,1024]{2,1,0:T(8,128)(2,1)}), bf16[8,8,1024]{2,1,0:T(8,128)(2,1)S(1)}, u32[]{:S(2)}, u32[]{:S(2)}) async-start(bf16[8,8,1024]{2,1,0:T(8,128)(2,1)} %net.1), calls=%async_computation.3 | async-start | bytes 262144 | tf_op jit(solution)/shard_map/all_to_all | solution.py:510
  54.6 1.0 %copy-start.1 = (f32[512,1,128]{2,1,0:T(1,128)S(1)}, f32[512,1,128]{2,1,0:T(1,128)}, u32[]{:S(2)}) copy-start(f32[512,1,128]{2,1,0:T(1,128)} %param.21) | copy-start | bytes 786436
  55.5 0.7 copy-start.3
  55.5 0.7 copy-start.4
  63.0 0.7 copy-start.5
  63.7 11.8 %all-to-all-start.1 = ((bf16[4,128,128]{2,1,0:T(8,128)(2,1)}), bf16[4,128,128]{2,1,0:T(8,128)(2,1)S(1)}, u32[]{:S(2)}, u32[]{:S(2)}) async-start(bf16[4,128,128]{2,1,0:T(8,128)(2,1)} %bitcast.7), calls=%async_computation.1 | async-start | bytes 262144 | tf_op jit(solution)/shard_map/all_to_all | solution.py:503
  69.0 0.7 copy-start.12
  75.5 0.6 copy-start.6
